TPU v7x, 32 devices: a whole 2x2x4 slice. The times are simulated.
32 devices in a mesh: cfg: 4 (over z), mode: 8 (over y, x, core).
Axes of the slice: x: 2, y: 2, z: 4, core: 2. Of those that a mesh axis runs over, the one named last changes fastest.
Arguments:
- coords: bfloat16 [10368, 2048], P('mode', 'cfg'), may hold values from -6 to 6
- curvature: float32 [10368], P('mode'), may hold values from 0.2 to 5
- weight: float32 [10368], P('mode'), may hold values from 0.3 to 3
- polar: bfloat16 [10368, 10368], P('mode'), may hold values from -0.078125 to 0.078125
- forces: bfloat16 [10368, 2048], P('mode', 'cfg'), may hold values from -6 to 6
Outputs:
- gradient: float32 [10368, 10368], P('cfg', 'mode')
All inputs are finite; a program needn't handle non-finite values.
Results may differ from a plain program's by a relative error of at most 0.019.
Values may be sent and summed in bfloat16 or wider, within the bound.
A program may use at most 192 MiB of HBM per device.

v0:
```python
import math

import jax
import jax.numpy as jnp
from jax import lax
from jax.sharding import PartitionSpec as P


def on_device(coords, curvature, weight, polar, forces):
    f32 = jnp.float32
    bf16 = jnp.bfloat16
    configs_dev = coords.shape[1]
    scaled = (coords.astype(f32) * curvature[:, None]).astype(bf16)
    weighted = (coords.astype(f32) * weight[:, None]).astype(bf16)
    contract = (((0,), (0,)), ((), ()))
    shares = lax.psum_scatter(
        lax.dot_general(polar, scaled, contract, preferred_element_type=f32).astype(jnp.bfloat16),
        "mode",
        scatter_dimension=0,
        tiled=True,
    ).astype(jnp.float32)
    resid_rows = (forces.astype(f32) + shares).astype(bf16)
    residual = lax.all_gather(resid_rows, "mode", axis=0, tiled=True)
    factor = 1.0 / math.sqrt(configs_dev * lax.axis_size("cfg"))
    across = (((1,), (1,)), ((), ()))
    return lax.psum_scatter(
        (lax.dot_general(residual, weighted, across, preferred_element_type=f32) * factor).astype(
            jnp.bfloat16
        ),
        "cfg",
        scatter_dimension=0,
        tiled=True,
    ).astype(jnp.float32)


def solution(mesh):
    placed = (P("mode", "cfg"), P("mode"), P("mode"), P("mode", None), P("mode", "cfg"))
    return jax.shard_map(
        on_device, mesh=mesh, in_specs=placed, out_specs=P("cfg", "mode"), check_vma=False
    )
```

profile of v0, /device:TPU:0, one launch (start us, length us, event | category | flops | bytes accessed | tf_op | source)
XLA Modules:
  0.0 746.0 jit_solution(12773726648723765596)
XLA Ops:
  6.5 0.0 reduce-scatter.5.cloned.1.call-start
  6.5 23.2 %fusion = bf16[10368,512]{1,0:T(8,128)(2,1)} fusion(bf16[1296,10368]{1,0:T(8,128)(2,1)} %param.8, bf16[1296,512]{1,0:T(8,128)(2,1)} %param.5, f32[1296]{0:T(1024)} %param.6), kind=kOutput, calls=%fused_computation.2 | convolution fusion | flops 13766713344 | bytes 38822976 | tf_op jit(solution)/shard_map/dot_general | solution.py:17
  29.7 0.0 copy-start
  29.7 0.0 reduce-scatter.5.cloned.1.call-update
  29.7 0.0 copy-start.1
  29.7 0.0 copy-start.2
  29.7 0.0 all-gather.2.cloned.1.call-start
  29.8 85.4 %reduce-scatter.5.cloned.1.call-done = bf16[1296,512]{1,0:T(8,128)(2,1)} async-done(((bf16[10368,512]{1,0:T(8,128)(2,1)}), bf16[1296,512]{1,0:T(8,128)(2,1)}) %reduce-scatter.5.cloned.1.call-update) | async-done | bytes 1327120 | tf_op jit(solution)/shard_map/reduce_scatter | solution.py:16
  115.2 0.0 copy-done
  115.2 2.7 add_convert_fusion
  117.9 0.0 all-gather.2.cloned.1.call-update
  118.0 0.2 reduce-scatter.7.cloned.1.call-start
  118.2 63.6 %all-gather.2.cloned.1.call-done = bf16[10368,512]{1,0:T(8,128)(2,1)} async-done(((bf16[1296,512]{1,0:T(8,128)(2,1)}), bf16[10368,512]{1,0:T(8,128)(2,1)}) %all-gather.2.cloned.1.call-update) | async-done | bytes 10616848 | tf_op jit(solution)/shard_map/all_gather | solution.py:23
  181.8 0.0 copy-done.1
  181.8 0.0 copy-done.2
  181.8 22.4 %multiply_convert_fusion = bf16[10368,1296]{0,1:T(8,128)(2,1)} fusion(bf16[10368,512]{1,0:T(8,128)(2,1)} %all-gather.2.cloned.1.call-done, bf16[1296,512]{1,0:T(8,128)(2,1)S(1)} %copy-done.1, f32[1296]{0:T(1024)S(1)} %copy-done.2), kind=kOutput, calls=%fused_computation | convolution fusion | flops 13788278784 | bytes 38822976 | tf_op jit(solution)/shard_map/dot_general | solution.py:27
  204.2 35.9 %copy.6 = bf16[10368,1296]{1,0:T(8,128)(2,1)} copy(bf16[10368,1296]{0,1:T(8,128)(2,1)} %multiply_convert_fusion) | data formatting | bytes 53747712
  240.1 0.0 reduce-scatter.7.cloned.1.call-update
  240.2 479.6 %reduce-scatter.7.cloned.1.call-done = bf16[2592,1296]{1,0:T(8,128)(2,1)} async-done(((bf16[10368,1296]{1,0:T(8,128)(2,1)}), bf16[2592,1296]{1,0:T(8,128)(2,1)}) %reduce-scatter.7.cloned.1.call-update) | async-done | bytes 6718480
  719.7 10.6 %copy.7 = bf16[2592,1296]{0,1:T(8,128)(2,1)} copy(bf16[2592,1296]{1,0:T(8,128)(2,1)} %reduce-scatter.7.cloned.1.call-done) | data formatting | bytes 13436928
  730.4 9.1 %convert_element_type.40 = f32[2592,1296]{0,1:T(8,128)} convert(bf16[2592,1296]{0,1:T(8,128)(2,1)} %copy.7) | non-fusion elementwise | flops 3359232 | bytes 20155392 | tf_op jit(solution)/shard_map/convert_element_type | solution.py:33
Async XLA Ops:
  6.5 108.7 %reduce-scatter.5.cloned.1.call-start = ((), (), s32[]{:S(2)}) async-start(), calls=%async_computation.2 | async-start | bytes 11943936 | tf_op jit(solution)/shard_map/reduce_scatter | solution.py:16
  29.7 85.5 %copy-start = (bf16[1296,512]{1,0:T(8,128)(2,1)S(1)}, bf16[1296,512]{1,0:T(8,128)(2,1)}, u32[]{:S(2)}) copy-start(bf16[1296,512]{1,0:T(8,128)(2,1)} %param.9) | copy-start | bytes 3981316
  29.7 152.1 %copy-start.1 = (bf16[1296,512]{1,0:T(8,128)(2,1)S(1)}, bf16[1296,512]{1,0:T(8,128)(2,1)}, u32[]{:S(2)}) copy-start(bf16[1296,512]{1,0:T(8,128)(2,1)} %param.5) | copy-start | bytes 3981316
  29.7 152.1 %copy-start.2 = (f32[1296]{0:T(1024)S(1)}, f32[1296]{0:T(1024)}, u32[]{:S(2)}) copy-start(f32[1296]{0:T(1024)} %param.7) | copy-start | bytes 15556
  29.7 152.0 %all-gather.2.cloned.1.call-start = ((), (), s32[]{:S(2)}) async-start(), calls=%async_computation.3 | async-start | bytes 11943936 | tf_op jit(solution)/shard_map/all_gather | solution.py:23
  118.0 601.7 %reduce-scatter.7.cloned.1.call-start = ((), (), s32[]{:S(2)}) async-start(), calls=%async_computation.4 | async-start | bytes 36495360
Sparse Core Ops, SparseCore 0:
  29.8 85.3 reduce-scatter.4
  118.1 63.6 all-gather.1
  240.3 479.3 reduce-scatter.6
where the time goes:
time: 747 us; the launch traced here: 746 us
  waiting for transfers between devices  629 us (84%)
  local copies, waits for them, and re-layouts  46.6 us (6%)
  matrix products  45.6 us (6%)
  between operations  13.1 us (2%)
  other arithmetic  11.8 us (2%)
    unnamed x4, waiting for transfers between devices  480 us
    reduce_scatter x1, waiting for transfers between devices, on_device(): lax.psum_scatter(lax.dot_general(polar, scaled, contract, preferred_eleme...  85.4 us
    all_gather x1, waiting for transfers between devices, on_device(): residual = lax.all_gather(resid_rows, 'mode', axis=0, tiled=True)  63.6 us
    unnamed x8, local copies, waits for them, and re-layouts  46.6 us
    dot_general x1, matrix products, on_device(): lax.dot_general(polar, scaled, contract, preferred_element_type=f32)  23.2 us
    dot_general x1, matrix products, on_device(): lax.dot_general(residual, weighted, across, preferred_element_type=f32)  22.4 us
  transfers between devices with their start and end apart: 3, of which 3 were waited for; matrix products, arithmetic and copies ran while one was open for 0% of the time, Pallas kernels for 0%

commit v1 on v0

v1 whole, which is shorter than its diff:
```python
import functools
import math

import jax
import jax.numpy as jnp
from jax import lax
from jax.experimental import pallas as pl
from jax.experimental.pallas import tpu as pltpu
from jax.sharding import PartitionSpec as P


def tile_of(extent, most):
    return max(t for t in range(8, most + 1, 8) if extent % t == 0)


def exchange_kernel(n, axis, step, whole, relative, x_ref, out_ref, send, recv, own):
    me = lax.axis_index(axis)
    here, rest = me // step, lax.rem(me, step)
    barrier = pltpu.get_barrier_semaphore()
    for d in range(1, n):
        target = lax.rem(here + d, n) * step + rest
        pl.semaphore_signal(
            barrier, inc=1, device_id={axis: target}, device_id_type=pl.DeviceIdType.MESH
        )
    pl.semaphore_wait(barrier, n - 1)
    copies = []
    for d in range(1, n):
        place = lax.rem(here + d, n)
        copies.append(
            pltpu.make_async_remote_copy(
                src_ref=x_ref if whole else x_ref.at[place],
                dst_ref=out_ref.at[n - d if relative else here],
                send_sem=send.at[d - 1],
                recv_sem=recv.at[d - 1],
                device_id={axis: place * step + rest},
                device_id_type=pl.DeviceIdType.MESH,
            )
        )
    local = pltpu.make_async_copy(
        x_ref if whole else x_ref.at[here], out_ref.at[0 if relative else here], own
    )
    for copy in copies:
        copy.start()
    local.start()
    local.wait()
    for copy in copies:
        copy.wait()


def exchange(x, axis, n, step, whole, relative, number):
    slab = x.shape if whole else x.shape[1:]
    return pl.pallas_call(
        functools.partial(exchange_kernel, n, axis, step, whole, relative),
        out_shape=jax.ShapeDtypeStruct((n, *slab), x.dtype),
        in_specs=[pl.BlockSpec(memory_space=pltpu.VMEM)],
        out_specs=pl.BlockSpec(memory_space=pl.ANY),
        scratch_shapes=[
            pltpu.SemaphoreType.DMA((n - 1,)),
            pltpu.SemaphoreType.DMA((n - 1,)),
            pltpu.SemaphoreType.DMA,
        ],
        cost_estimate=pl.CostEstimate(flops=0, bytes_accessed=150_000_000, transcendentals=0),
        compiler_params=pltpu.CompilerParams(
            collective_id=number, has_side_effects=True, vmem_limit_bytes=16 * 1024 * 1024
        ),
    )(x)


def share_kernel(scaled, polar, out):
    block = lax.dot_general(
        scaled[...], polar[...], (((1,), (0,)), ((), ())), preferred_element_type=jnp.float32
    ).astype(out.dtype)
    width = out.shape[2]
    for q in range(out.shape[0]):
        out[q] = block[q * width : (q + 1) * width].T


def share(scaled, polar, n):
    configs_dev, rows = scaled.shape
    whole = polar.shape[1]
    tile = max(t for t in range(128, 1153, 128) if whole % t == 0)
    return pl.pallas_call(
        share_kernel,
        grid=(whole // tile,),
        out_shape=jax.ShapeDtypeStruct((n, whole, configs_dev // n), polar.dtype),
        in_specs=[
            pl.BlockSpec((configs_dev, rows), lambda i: (0, 0)),
            pl.BlockSpec((rows, tile), lambda i: (0, i)),
        ],
        out_specs=pl.BlockSpec((n, tile, configs_dev // n), lambda i: (0, i, 0)),
        compiler_params=pltpu.CompilerParams(vmem_limit_bytes=40 * 1024 * 1024),
    )(scaled, polar)


def product_kernel(factor, per, resid, weights, out):
    across = (((1,), (1,)), ((), ()))
    n_mode, n, rows, _ = resid.shape
    for h in range(per):
        total = 0.0
        for d in range(n):
            block = jnp.concatenate([resid[j, d] for j in range(h, n_mode, per)], axis=1)
            total = total + lax.dot_general(
                weights[d], block, across, preferred_element_type=jnp.float32
            )
        out[:, h * rows : (h + 1) * rows] = total * factor


def product(resid, weights, per, factor):
    n_mode, n, rows, width = resid.shape
    cols, configs_dev = weights.shape[1:]
    tile = tile_of(cols, 224)
    return pl.pallas_call(
        functools.partial(product_kernel, factor, per),
        grid=(cols // tile,),
        out_shape=jax.ShapeDtypeStruct((cols, per * rows), jnp.float32),
        in_specs=[
            pl.BlockSpec((n_mode, n, rows, width), lambda i: (0, 0, 0, 0)),
            pl.BlockSpec((n, tile, configs_dev), lambda i: (0, i, 0)),
        ],
        out_specs=pl.BlockSpec((tile, per * rows), lambda i: (i, 0)),
        compiler_params=pltpu.CompilerParams(vmem_limit_bytes=56 * 1024 * 1024),
    )(resid, weights)


def on_device(coords, curvature, weight, polar, forces):
    f32 = jnp.float32
    bf16 = jnp.bfloat16
    n_cfg, n_mode = lax.axis_size("cfg"), lax.axis_size("mode")
    per = n_mode // n_cfg
    rows, configs_dev = coords.shape
    width = configs_dev // n_cfg
    factor = 1.0 / math.sqrt(configs_dev * n_cfg)
    scaled = (coords.astype(f32) * curvature[:, None]).astype(bf16)
    weighted = (coords.astype(f32) * weight[:, None]).astype(bf16)
    part = share(scaled.T, polar, n_cfg)
    part = part.reshape(n_cfg, n_cfg, per, rows, width).transpose(0, 2, 1, 3, 4)
    part = part.reshape(n_mode * n_cfg * rows, width)
    part, weighted, forces = lax.optimization_barrier((part, weighted, forces))
    shares = lax.psum_scatter(
        part, "mode", scatter_dimension=0, tiled=True
    ).reshape(n_cfg, rows, width)
    weights = exchange(weighted, "cfg", n_cfg, 1, True, True, 0)
    pushes = exchange(
        forces.reshape(rows, n_cfg, width).transpose(1, 0, 2), "mode", n_cfg, per, False, False, 1
    )
    pushes, weights = lax.optimization_barrier((pushes, weights))
    mine = (pushes.astype(f32) + shares.astype(f32)).astype(bf16)
    mine = exchange(mine, "cfg", n_cfg, 1, False, True, 2)
    resid = lax.all_gather(
        mine.reshape(n_cfg * rows, width), "mode", axis=0, tiled=True
    ).reshape(n_mode, n_cfg, rows, width)
    return product(resid, weights, per, factor).T


def solution(mesh):
    placed = (P("mode", "cfg"), P("mode"), P("mode"), P("mode", None), P("mode", "cfg"))
    return jax.shard_map(
        on_device, mesh=mesh, in_specs=placed, out_specs=P("cfg", "mode"), check_vma=False
    )
```

time: 747 us -> 309 us (0.41)
  waiting for transfers between devices: 629 us -> 69.1 us
  Pallas kernels: 0 us -> 212 us
  matrix products: 45.6 us -> 0 us
  local copies, waits for them, and re-layouts: 46.6 us -> 8.97 us
    unnamed x4 -> x2, waiting for transfers between devices: 480 us -> 0.03 us
    pallas_call x0 -> x5, Pallas kernels: none -> 212 us  [the longest x3 163 us: exchange(): pl.pallas_call(functools.partial(exchange_kernel, n, axis, step, whole, r...]
    reduce_scatter x1, waiting for transfers between devices: 85.4 us -> 0.01 us  [on_device(): lax.psum_scatter(part, 'mode', scatter_dimension=0, tiled=True)]
    dot_general x2 -> x0, matrix products: 45.6 us -> none  [the longest x1 23.2 us: on_device(): lax.dot_general(polar, scaled, contract, preferred_element_type=f32)]
    unnamed x8 -> x6, local copies, waits for them, and re-layouts: 46.6 us -> 2.38 us
  transfers between devices with their start and end apart: 3 -> 2, of which waited for: 3 -> 1; matrix products, arithmetic and copies ran while one was open for 0% -> 0% of each run, Pallas kernels for 0% -> 35%
where the time goes in v1:
time: 309 us
  Pallas kernels  212 us (69%)
  waiting for transfers between devices  69.1 us (22%)
  between operations  13.5 us (4%)
  local copies, waits for them, and re-layouts  8.97 us (3%)
  other arithmetic  5.02 us (2%)
    pallas_call x3, Pallas kernels, exchange(): pl.pallas_call(functools.partial(exchange_kernel, n, axis, step, whole, r...  163 us
    all_gather x1, waiting for transfers between devices, on_device(): lax.all_gather(mine.reshape(n_cfg * rows, width), 'mode', axis=0, tiled=T...  69.1 us
    pallas_call x1, Pallas kernels, product(): pl.pallas_call(functools.partial(product_kernel, factor, per), grid=(cols...  27 us
    pallas_call x1, Pallas kernels, share(): pl.pallas_call(share_kernel, grid=(whole // tile,), out_shape=jax.ShapeDt...  22.6 us
  transfers between devices with their start and end apart: 2, of which 1 were waited for; matrix products, arithmetic and copies ran while one was open for 0% of the time, Pallas kernels for 35%

profile of v1, /device:TPU:0, one launch (start us, length us, event | category | flops | bytes accessed | tf_op | source)
XLA Modules:
  0.0 309.1 jit_solution(9854897558040966959)
XLA Ops:
  6.5 0.0 copy-start
  6.5 0.0 reduce-scatter.2.cloned.1.call-start
  6.5 3.4 %fusion.1 = (bf16[1296,512]{1,0:T(8,128)(2,1)}, bf16[512,1296]{0,1:T(8,128)(2,1)}) fusion(bf16[1296,512]{1,0:T(8,128)(2,1)} %param.5, f32[1296]{0:T(1024)} %param.7, f32[1296]{0:T(1024)} %param.6), kind=kLoop, calls=%fused_computation.3 | loop fusion | flops 3317760 | bytes 3991680 | tf_op jit(solution)/shard_map/convert_element_type | solution.py:134
  9.9 1.8 copy.8.scaled
  11.7 22.6 %shard_map.55 = bf16[4,10368,128]{2,1,0:T(8,128)(2,1)S(1)} custom-call(bf16[512,1296]{1,0:T(8,128)(2,1)S(1)} %copy.8.scaled, bf16[1296,10368]{1,0:T(8,128)(2,1)} %polar.1), custom_call_target="tpu_custom_call" | custom-call | tf_op jit(solution)/shard_map/pallas_call | solution.py:82
  34.3 4.6 %copy.9 = bf16[4,2,4,1296,128]{4,3,2,1,0:T(8,128)(2,1)} copy(bf16[4,2,4,1296,128]{4,3,1,2,0:T(8,128)(2,1)S(1)} %bitcast.18) | data formatting | bytes 21233664 | tf_op jit(solution)/shard_map/transpose | solution.py:136
  38.9 0.0 reduce-scatter.2.cloned.1.call-update
  38.9 0.0 all-gather.2.cloned.1.call-start
  39.0 0.0 copy-done
  39.0 0.2 bitcast_bitcast_fusion.x_ref
  39.2 0.0 copy-start.2
  39.2 19.2 %shard_map.56 = bf16[4,1296,128]{2,1,0:T(8,128)(2,1)S(1)} custom-call(bf16[4,1296,128]{2,1,0:T(8,128)(2,1)S(1)} %bitcast_bitcast_fusion.x_ref), custom_call_target="tpu_custom_call" | custom-call | bytes 150000000 | tf_op jit(solution)/shard_map/pallas_call | solution.py:52
  58.5 0.0 copy-done.2
  58.5 90.1 %shard_map.57.weights = bf16[4,1296,512]{2,1,0:T(8,128)(2,1)S(1)} custom-call(bf16[1296,512]{1,0:T(8,128)(2,1)S(1)} %copy-done.2), custom_call_target="tpu_custom_call" | custom-call | bytes 150000000 | tf_op jit(solution)/shard_map/pallas_call | solution.py:52
  148.6 0.0 copy-start.1
  148.6 2.4 copy-done.1
  151.0 0.0 reduce-scatter.2.cloned.1.call-done
  151.0 1.7 fusion.2.x_ref
  152.6 53.5 %shard_map.58 = bf16[4,1296,128]{2,1,0:T(8,128)(2,1)} custom-call(bf16[4,1296,128]{2,1,0:T(8,128)(2,1)S(1)} %fusion.2.x_ref), custom_call_target="tpu_custom_call" | custom-call | bytes 150000000 | tf_op jit(solution)/shard_map/pallas_call | solution.py:52
  206.2 0.0 all-gather.2.cloned.1.call-update
  206.2 69.1 %all-gather.2.cloned.1.call-done = bf16[41472,128]{1,0:T(8,128)(2,1)} async-done(((bf16[5184,128]{1,0:T(8,128)(2,1)}), bf16[41472,128]{1,0:T(8,128)(2,1)}) %all-gather.2.cloned.1.call-update) | async-done | bytes 10616848 | tf_op jit(solution)/shard_map/all_gather | solution.py:149
  275.3 27.0 %shard_map.59 = f32[1296,2592]{1,0:T(8,128)} custom-call(bf16[8,4,1296,128]{3,2,1,0:T(8,128)(2,1)} %bitcast.20, bf16[4,1296,512]{2,1,0:T(8,128)(2,1)} %copy-done.1), custom_call_target="tpu_custom_call" | custom-call | tf_op jit(solution)/shard_map/pallas_call | solution.py:112
Async XLA Ops:
  6.5 32.4 %copy-start = (bf16[1296,512]{1,0:T(8,128)(2,1)S(1)}, bf16[1296,512]{1,0:T(8,128)(2,1)}, u32[]{:S(2)}) copy-start(bf16[1296,512]{1,0:T(8,128)(2,1)} %param.9) | copy-start | bytes 3981316
  6.5 144.4 %reduce-scatter.2.cloned.1.call-start = ((), (), s32[]{:S(2)}) async-start(), calls=%async_computation.1 | async-start | bytes 11943936 | tf_op jit(solution)/shard_map/reduce_scatter | solution.py:139
  38.9 236.3 %all-gather.2.cloned.1.call-start = ((), (), s32[]{:S(2)}) async-start(), calls=%async_computation.2 | async-start | bytes 11943936 | tf_op jit(solution)/shard_map/all_gather | solution.py:149
  39.2 19.3 %copy-start.2 = (bf16[1296,512]{1,0:T(8,128)(2,1)S(1)}, bf16[1296,512]{1,0:T(8,128)(2,1)}, u32[]{:S(2)}) copy-start(bf16[1296,512]{1,0:T(8,128)(2,1)} %get-tuple-element.11.x_ref) | copy-start | bytes 3981316
  148.6 2.4 copy-start.1
Sparse Core Ops, SparseCore 0:
  39.0 85.3 reduce-scatter.1
  206.3 68.8 all-gather.1

commit v2 on v1

--- a/solution.py
+++ b/solution.py
@@ -92,22 +92,24 @@
     )(scaled, polar)
 
 
-def product_kernel(factor, per, resid, weights, out):
+def product_kernel(factor, per, resid, early, late, out):
     across = (((1,), (1,)), ((), ()))
     n_mode, n, rows, _ = resid.shape
+    first = early.shape[2]
     for h in range(per):
         total = 0.0
         for d in range(n):
             block = jnp.concatenate([resid[j, d] for j in range(h, n_mode, per)], axis=1)
-            total = total + lax.dot_general(
-                weights[d], block, across, preferred_element_type=jnp.float32
-            )
+            for weights, cut in ((early, block[:, :first]), (late, block[:, first:])):
+                total = total + lax.dot_general(
+                    weights[d], cut, across, preferred_element_type=jnp.float32
+                )
         out[:, h * rows : (h + 1) * rows] = total * factor
 
 
-def product(resid, weights, per, factor):
+def product(resid, early, late, per, factor):
     n_mode, n, rows, width = resid.shape
-    cols, configs_dev = weights.shape[1:]
+    cols = early.shape[1]
     tile = tile_of(cols, 224)
     return pl.pallas_call(
         functools.partial(product_kernel, factor, per),
@@ -115,11 +117,12 @@
         out_shape=jax.ShapeDtypeStruct((cols, per * rows), jnp.float32),
         in_specs=[
             pl.BlockSpec((n_mode, n, rows, width), lambda i: (0, 0, 0, 0)),
-            pl.BlockSpec((n, tile, configs_dev), lambda i: (0, i, 0)),
+            pl.BlockSpec((n, tile, early.shape[2]), lambda i: (0, i, 0)),
+            pl.BlockSpec((n, tile, late.shape[2]), lambda i: (0, i, 0)),
         ],
         out_specs=pl.BlockSpec((tile, per * rows), lambda i: (i, 0)),
         compiler_params=pltpu.CompilerParams(vmem_limit_bytes=56 * 1024 * 1024),
-    )(resid, weights)
+    )(resid, early, late)
 
 
 def on_device(coords, curvature, weight, polar, forces):
@@ -139,17 +142,20 @@
     shares = lax.psum_scatter(
         part, "mode", scatter_dimension=0, tiled=True
     ).reshape(n_cfg, rows, width)
-    weights = exchange(weighted, "cfg", n_cfg, 1, True, True, 0)
+    first = configs_dev * 3 // 4
+    early = exchange(weighted[:, :first], "cfg", n_cfg, 1, True, True, 0)
     pushes = exchange(
         forces.reshape(rows, n_cfg, width).transpose(1, 0, 2), "mode", n_cfg, per, False, False, 1
     )
-    pushes, weights = lax.optimization_barrier((pushes, weights))
+    pushes, early = lax.optimization_barrier((pushes, early))
     mine = (pushes.astype(f32) + shares.astype(f32)).astype(bf16)
     mine = exchange(mine, "cfg", n_cfg, 1, False, True, 2)
+    mine, rest = lax.optimization_barrier((mine, weighted[:, first:]))
+    late = exchange(rest, "cfg", n_cfg, 1, True, True, 3)
     resid = lax.all_gather(
         mine.reshape(n_cfg * rows, width), "mode", axis=0, tiled=True
     ).reshape(n_mode, n_cfg, rows, width)
-    return product(resid, weights, per, factor).T
+    return product(resid, early, late, per, factor).T
 
 
 def solution(mesh):

time: 309 us -> 289 us (0.935)
  waiting for transfers between devices: 69.1 us -> 37.6 us
  Pallas kernels: 212 us -> 221 us
    all_gather x1, waiting for transfers between devices: 69.1 us -> 37.6 us  [on_device(): lax.all_gather(mine.reshape(n_cfg * rows, width), 'mode', axis=0, tiled=T...]
    pallas_call x1, Pallas kernels: 27 us -> 33.7 us  [product(): pl.pallas_call(functools.partial(product_kernel, factor, per), grid=(cols...]
    pallas_call x3 -> x4, Pallas kernels: 163 us -> 165 us  [exchange(): pl.pallas_call(functools.partial(exchange_kernel, n, axis, step, whole, r...]
  transfers between devices with their start and end apart: 2 -> 2, of which waited for: 1 -> 1; matrix products, arithmetic and copies ran while one was open for 0% -> 0% of each run, Pallas kernels for 35% -> 41%
where the time goes in v2:
time: 289 us; the launch traced here: 288 us
  Pallas kernels  221 us (76%)
  waiting for transfers between devices  37.6 us (13%)
  between operations  13.5 us (5%)
  local copies, waits for them, and re-layouts  11.1 us (4%)
  other arithmetic  5.05 us (2%)
    pallas_call x4, Pallas kernels, exchange(): pl.pallas_call(functools.partial(exchange_kernel, n, axis, step, whole, r...  165 us
    all_gather x1, waiting for transfers between devices, on_device(): lax.all_gather(mine.reshape(n_cfg * rows, width), 'mode', axis=0, tiled=T...  37.6 us
    pallas_call x1, Pallas kernels, product(): pl.pallas_call(functools.partial(product_kernel, factor, per), grid=(cols...  33.7 us
    pallas_call x1, Pallas kernels, share(): pl.pallas_call(share_kernel, grid=(whole // tile,), out_shape=jax.ShapeDt...  22.6 us
  transfers between devices with their start and end apart: 2, of which 1 were waited for; matrix products, arithmetic and copies ran while one was open for 0% of the time, Pallas kernels for 41%

profile of v2, /device:TPU:0, one launch (start us, length us, event | category | flops | bytes accessed | tf_op | source)
XLA Modules:
  0.0 288.4 jit_solution(10364268508222279770)
XLA Ops:
  6.5 0.0 copy-start
  6.5 0.0 reduce-scatter.2.cloned.1.call-start
  6.5 3.4 %fusion.1 = (bf16[1296,512]{1,0:T(8,128)(2,1)}, bf16[512,1296]{0,1:T(8,128)(2,1)}) fusion(bf16[1296,512]{1,0:T(8,128)(2,1)} %param.5, f32[1296]{0:T(1024)} %param.7, f32[1296]{0:T(1024)} %param.6), kind=kLoop, calls=%fused_computation.3 | loop fusion | flops 3317760 | bytes 3991680 | tf_op jit(solution)/shard_map/convert_element_type | solution.py:137
  9.9 1.8 copy.8.scaled
  11.7 22.6 %shard_map.55 = bf16[4,10368,128]{2,1,0:T(8,128)(2,1)S(1)} custom-call(bf16[512,1296]{1,0:T(8,128)(2,1)S(1)} %copy.8.scaled, bf16[1296,10368]{1,0:T(8,128)(2,1)} %polar.1), custom_call_target="tpu_custom_call" | custom-call | tf_op jit(solution)/shard_map/pallas_call | solution.py:82
  34.3 4.6 %copy.9 = bf16[4,2,4,1296,128]{4,3,2,1,0:T(8,128)(2,1)} copy(bf16[4,2,4,1296,128]{4,3,1,2,0:T(8,128)(2,1)S(1)} %bitcast.18) | data formatting | bytes 21233664 | tf_op jit(solution)/shard_map/transpose | solution.py:139
  38.9 0.0 reduce-scatter.2.cloned.1.call-update
  38.9 0.0 all-gather.2.cloned.1.call-start
  39.0 1.2 copy-done.3
  40.3 0.1 slice.6.x_ref
  40.4 0.0 copy-done
  40.4 0.2 bitcast_bitcast_fusion.x_ref
  40.6 19.2 %shard_map.56 = bf16[4,1296,128]{2,1,0:T(8,128)(2,1)S(1)} custom-call(bf16[4,1296,128]{2,1,0:T(8,128)(2,1)S(1)} %bitcast_bitcast_fusion.x_ref), custom_call_target="tpu_custom_call" | custom-call | bytes 150000000 | tf_op jit(solution)/shard_map/pallas_call | solution.py:52
  59.9 68.8 %shard_map.57.early = bf16[4,1296,384]{2,1,0:T(8,128)(2,1)S(1)} custom-call(bf16[1296,384]{1,0:T(8,128)(2,1)S(1)} %slice.6.x_ref), custom_call_target="tpu_custom_call" | custom-call | bytes 150000000 | tf_op jit(solution)/shard_map/pallas_call | solution.py:52
  128.7 0.0 copy-start.1
  128.7 2.0 copy-done.1
  130.7 1.7 fusion.2.x_ref
  132.3 46.4 %shard_map.58 = bf16[4,1296,128]{2,1,0:T(8,128)(2,1)} custom-call(bf16[4,1296,128]{2,1,0:T(8,128)(2,1)S(1)} %fusion.2.x_ref), custom_call_target="tpu_custom_call" | custom-call | bytes 150000000 | tf_op jit(solution)/shard_map/pallas_call | solution.py:52
  178.8 0.0 all-gather.2.cloned.1.call-update
  178.8 30.4 %shard_map.59.late = bf16[4,1296,128]{2,1,0:T(8,128)(2,1)S(1)} custom-call(bf16[1296,128]{1,0:T(8,128)(2,1)S(1)} %slice.7.x_ref), custom_call_target="tpu_custom_call" | custom-call | bytes 150000000 | tf_op jit(solution)/shard_map/pallas_call | solution.py:52
  209.2 0.0 copy-start.2
  209.2 1.1 copy-done.2
  210.3 37.6 %all-gather.2.cloned.1.call-done = bf16[41472,128]{1,0:T(8,128)(2,1)} async-done(((bf16[5184,128]{1,0:T(8,128)(2,1)}), bf16[41472,128]{1,0:T(8,128)(2,1)}) %all-gather.2.cloned.1.call-update) | async-done | bytes 10616848 | tf_op jit(solution)/shard_map/all_gather | solution.py:155
  247.8 33.7 %shard_map.60 = f32[1296,2592]{1,0:T(8,128)} custom-call(bf16[8,4,1296,128]{3,2,1,0:T(8,128)(2,1)} %bitcast.20, bf16[4,1296,384]{2,1,0:T(8,128)(2,1)} %copy-done.1, bf16[4,1296,128]{2,1,0:T(8,128)(2,1)} %copy-done.2), custom_call_target="tpu_custom_call" | custom-call | tf_op jit(solution)/shard_map/pallas_call | solution.py:114
  (3 shorter events, 0.0 us)
Async XLA Ops:
  6.5 33.9 %copy-start = (bf16[1296,512]{1,0:T(8,128)(2,1)S(1)}, bf16[1296,512]{1,0:T(8,128)(2,1)}, u32[]{:S(2)}) copy-start(bf16[1296,512]{1,0:T(8,128)(2,1)} %param.9) | copy-start | bytes 3981316
  6.5 124.1 %reduce-scatter.2.cloned.1.call-start = ((), (), s32[]{:S(2)}) async-start(), calls=%async_computation.1 | async-start | bytes 11943936 | tf_op jit(solution)/shard_map/reduce_scatter | solution.py:142
  38.9 1.3 copy-start.3
  38.9 208.9 %all-gather.2.cloned.1.call-start = ((), (), s32[]{:S(2)}) async-start(), calls=%async_computation.2 | async-start | bytes 11943936 | tf_op jit(solution)/shard_map/all_gather | solution.py:155
  128.7 2.0 copy-start.1
  209.2 1.1 copy-start.2
Sparse Core Ops, SparseCore 0:
  39.1 85.3 reduce-scatter.1
  178.9 68.8 all-gather.1

commit v3 on v2

--- a/solution.py
+++ b/solution.py
@@ -142,7 +142,7 @@
     shares = lax.psum_scatter(
         part, "mode", scatter_dimension=0, tiled=True
     ).reshape(n_cfg, rows, width)
-    first = configs_dev * 3 // 4
+    first = configs_dev // 2
     early = exchange(weighted[:, :first], "cfg", n_cfg, 1, True, True, 0)
     pushes = exchange(
         forces.reshape(rows, n_cfg, width).transpose(1, 0, 2), "mode", n_cfg, per, False, False, 1

time: 289 us -> 256 us (0.89)
  Pallas kernels: 221 us -> 196 us
  waiting for transfers between devices: 37.6 us -> 31.8 us
    all_gather x1, waiting for transfers between devices: 37.6 us -> 14.9 us  [on_device(): lax.all_gather(mine.reshape(n_cfg * rows, width), 'mode', axis=0, tiled=T...]
    pallas_call x4, Pallas kernels: 165 us -> 146 us  [exchange(): pl.pallas_call(functools.partial(exchange_kernel, n, axis, step, whole, r...]
    reduce_scatter x1, waiting for transfers between devices: 0.01 us -> 16.8 us  [on_device(): lax.psum_scatter(part, 'mode', scatter_dimension=0, tiled=True)]
    pallas_call x1, Pallas kernels: 33.7 us -> 27.4 us  [product(): pl.pallas_call(functools.partial(product_kernel, factor, per), grid=(cols...]
  transfers between devices with their start and end apart: 2 -> 2, of which waited for: 1 -> 2; matrix products, arithmetic and copies ran while one was open for 0% -> 0% of each run, Pallas kernels for 41% -> 47%
where the time goes in v3:
time: 256 us
  Pallas kernels  196 us (77%)
  waiting for transfers between devices  31.8 us (12%)
  between operations  13.5 us (5%)
  local copies, waits for them, and re-layouts  9.74 us (4%)
  other arithmetic  5.05 us (2%)
    pallas_call x4, Pallas kernels, exchange(): pl.pallas_call(functools.partial(exchange_kernel, n, axis, step, whole, r...  146 us
    pallas_call x1, Pallas kernels, product(): pl.pallas_call(functools.partial(product_kernel, factor, per), grid=(cols...  27.4 us
    pallas_call x1, Pallas kernels, share(): pl.pallas_call(share_kernel, grid=(whole // tile,), out_shape=jax.ShapeDt...  22.6 us
    reduce_scatter x1, waiting for transfers between devices, on_device(): lax.psum_scatter(part, 'mode', scatter_dimension=0, tiled=True)  16.8 us
    all_gather x1, waiting for transfers between devices, on_device(): lax.all_gather(mine.reshape(n_cfg * rows, width), 'mode', axis=0, tiled=T...  14.9 us
  transfers between devices with their start and end apart: 2, of which 2 were waited for; matrix products, arithmetic and copies ran while one was open for 0% of the time, Pallas kernels for 47%

profile of v3, /device:TPU:0, one launch (start us, length us, event | category | flops | bytes accessed | tf_op | source)
XLA Modules:
  0.0 256.0 jit_solution(3481098568234945173)
XLA Ops:
  6.5 0.0 copy-start
  6.5 0.0 reduce-scatter.2.cloned.1.call-start
  6.5 3.4 %fusion.1 = (bf16[1296,512]{1,0:T(8,128)(2,1)}, bf16[512,1296]{0,1:T(8,128)(2,1)}) fusion(bf16[1296,512]{1,0:T(8,128)(2,1)} %param.5, f32[1296]{0:T(1024)} %param.7, f32[1296]{0:T(1024)} %param.6), kind=kLoop, calls=%fused_computation.3 | loop fusion | flops 3317760 | bytes 3991680 | tf_op jit(solution)/shard_map/convert_element_type | solution.py:137
  9.9 1.8 copy.8.scaled
  11.7 22.6 %shard_map.55 = bf16[4,10368,128]{2,1,0:T(8,128)(2,1)S(1)} custom-call(bf16[512,1296]{1,0:T(8,128)(2,1)S(1)} %copy.8.scaled, bf16[1296,10368]{1,0:T(8,128)(2,1)} %polar.1), custom_call_target="tpu_custom_call" | custom-call | tf_op jit(solution)/shard_map/pallas_call | solution.py:82
  34.3 4.6 %copy.9 = bf16[4,2,4,1296,128]{4,3,2,1,0:T(8,128)(2,1)} copy(bf16[4,2,4,1296,128]{4,3,1,2,0:T(8,128)(2,1)S(1)} %bitcast.18) | data formatting | bytes 21233664 | tf_op jit(solution)/shard_map/transpose | solution.py:139
  38.9 0.0 reduce-scatter.2.cloned.1.call-update
  38.9 0.0 all-gather.2.cloned.1.call-start
  39.0 0.0 copy-done
  39.0 0.2 bitcast_bitcast_fusion.x_ref
  39.2 0.0 copy-start.3
  39.2 19.2 %shard_map.56 = bf16[4,1296,128]{2,1,0:T(8,128)(2,1)S(1)} custom-call(bf16[4,1296,128]{2,1,0:T(8,128)(2,1)S(1)} %bitcast_bitcast_fusion.x_ref), custom_call_target="tpu_custom_call" | custom-call | bytes 150000000 | tf_op jit(solution)/shard_map/pallas_call | solution.py:52
  58.5 0.0 copy-done.3
  58.5 0.1 fusion.4
  58.6 47.4 %shard_map.57.early = bf16[4,1296,256]{2,1,0:T(8,128)(2,1)S(1)} custom-call(bf16[1296,256]{1,0:T(8,128)(2,1)S(1)} %get-tuple-element.20.x_ref), custom_call_target="tpu_custom_call" | custom-call | bytes 150000000 | tf_op jit(solution)/shard_map/pallas_call | solution.py:52
  106.0 1.6 copy-done.1
  107.6 16.8 %reduce-scatter.2.cloned.1.call-done = bf16[5184,128]{1,0:T(8,128)(2,1)} async-done(((bf16[41472,128]{1,0:T(8,128)(2,1)}), bf16[5184,128]{1,0:T(8,128)(2,1)}) %reduce-scatter.2.cloned.1.call-update) | async-done | bytes 1327120 | tf_op jit(solution)/shard_map/reduce_scatter | solution.py:142
  124.4 1.7 fusion.2.x_ref
  126.1 25.8 %shard_map.58 = bf16[4,1296,128]{2,1,0:T(8,128)(2,1)} custom-call(bf16[4,1296,128]{2,1,0:T(8,128)(2,1)S(1)} %fusion.2.x_ref), custom_call_target="tpu_custom_call" | custom-call | bytes 150000000 | tf_op jit(solution)/shard_map/pallas_call | solution.py:52
  151.9 0.0 all-gather.2.cloned.1.call-update
  151.9 53.4 %shard_map.59.late = bf16[4,1296,256]{2,1,0:T(8,128)(2,1)S(1)} custom-call(bf16[1296,256]{1,0:T(8,128)(2,1)S(1)} %get-tuple-element.18.x_ref), custom_call_target="tpu_custom_call" | custom-call | bytes 150000000 | tf_op jit(solution)/shard_map/pallas_call | solution.py:52
  205.3 1.5 copy-done.2
  206.8 14.9 %all-gather.2.cloned.1.call-done = bf16[41472,128]{1,0:T(8,128)(2,1)} async-done(((bf16[5184,128]{1,0:T(8,128)(2,1)}), bf16[41472,128]{1,0:T(8,128)(2,1)}) %all-gather.2.cloned.1.call-update) | async-done | bytes 10616848 | tf_op jit(solution)/shard_map/all_gather | solution.py:155
  221.7 27.4 %shard_map.60 = f32[1296,2592]{1,0:T(8,128)} custom-call(bf16[8,4,1296,128]{3,2,1,0:T(8,128)(2,1)} %bitcast.20, bf16[4,1296,256]{2,1,0:T(8,128)(2,1)} %copy-done.1, bf16[4,1296,256]{2,1,0:T(8,128)(2,1)} %copy-done.2), custom_call_target="tpu_custom_call" | custom-call | tf_op jit(solution)/shard_map/pallas_call | solution.py:114
  (2 shorter events, 0.0 us)
Async XLA Ops:
  6.5 32.5 %copy-start = (bf16[1296,512]{1,0:T(8,128)(2,1)S(1)}, bf16[1296,512]{1,0:T(8,128)(2,1)}, u32[]{:S(2)}) copy-start(bf16[1296,512]{1,0:T(8,128)(2,1)} %param.9) | copy-start | bytes 3981316
  6.5 117.9 %reduce-scatter.2.cloned.1.call-start = ((), (), s32[]{:S(2)}) async-start(), calls=%async_computation.1 | async-start | bytes 11943936 | tf_op jit(solution)/shard_map/reduce_scatter | solution.py:142
  38.9 182.8 %all-gather.2.cloned.1.call-start = ((), (), s32[]{:S(2)}) async-start(), calls=%async_computation.2 | async-start | bytes 11943936 | tf_op jit(solution)/shard_map/all_gather | solution.py:155
  39.2 19.3 %copy-start.3 = (bf16[1296,512]{1,0:T(8,128)(2,1)S(1)}, bf16[1296,512]{1,0:T(8,128)(2,1)}, u32[]{:S(2)}) copy-start(bf16[1296,512]{1,0:T(8,128)(2,1)} %get-tuple-element.13) | copy-start | bytes 3981316
  106.0 1.6 copy-start.1
  205.3 1.5 copy-start.2
Sparse Core Ops, SparseCore 0:
  39.1 85.3 reduce-scatter.1
  152.0 69.6 all-gather.1
